TPU v7x, 128 devices: a whole 4x4x4 slice. The times are simulated.
128 devices in a mesh: blk: 8 (over y, z_lo), mode: 16 (over z_hi, x, core).
Axes of the slice: x: 4, y: 4, z: 4 (z_hi: 2, z_lo: 2; z = z_hi * 2 + z_lo), core: 2. Of those that a mesh axis runs over, the one named last changes fastest.
Arguments:
- density: bfloat16 [2, 256, 2048, 256], P(None, 'mode', 'blk'), may hold values from -6 to 6
- kernel_tiles: bfloat16 [256, 16, 8, 2, 128, 128], P('mode', 'blk'), may hold values from -0.125 to 0.125
- tile_index: int32 [256, 16, 8], P('mode', 'blk'), may hold values from 0 to 1
- coupling: bfloat16 [2, 9, 256, 2048], P(None, None, 'mode', 'blk'), may hold values from -4 to 4
- spread: int32 [2048], P('blk'), may hold values from 0 to 4
- liner: int32 [2048], P('blk'), may hold values 0 or 1
Outputs:
- applied: bfloat16 [2, 256, 2048, 256], P(None, 'mode', 'blk')
Inputs may be any that keep to these rules, and one draw needn't show every extreme that they name: `tile_index`: each retained tile names one column tile of its source shard.
All inputs are finite; a program needn't handle non-finite values. No bound on the sum of `liner` on one device may be relied on, other than what follows from the above.
Results may differ from a plain program's by a relative error of at most 0.0033.
Values may be sent and summed in bfloat16 or wider, within the bound.
No kernel may reach another device: no remote copies, remote signals or barrier semaphores. Data moves between devices by JAX's collectives and lax.ppermute only.
A program may use at most 320 MiB of HBM per device.

v0:
```python
import functools

import jax
import jax.numpy as jnp
from jax import lax
from jax.experimental import pallas as pl
from jax.experimental.pallas import tpu as pltpu
from jax.sharding import PartitionSpec as P


TILE = 128
ROLES = ((0, 1, 2), (1, 2, 0), (2, 0, 1))

GROUPS = (((1,), (1,), (1,)), ((3, 1), (3, 1), (4, 1)))


def blk_of(node):
    gray = node & 3
    return (gray ^ (gray >> 1)) * 2 + (node >> 2)


def node_of(blk):
    y = blk // 2
    return (y ^ (y >> 1)) | ((blk % 2) << 2)


def swap(block, direction):
    pairs = [(blk_of(node), blk_of(node ^ (1 << direction))) for node in range(8)]
    return lax.ppermute(block, "blk", pairs)


def near_rows(index_ref, shard_ref, first, row, kernels, density_refs):
    left, right = [], []
    for slot, density_ref in enumerate(density_refs):
        tile = index_ref[first + row * 8 + shard_ref[slot]]
        at = pl.ds(pl.multiple_of(tile * TILE, TILE), TILE)
        right.append(jnp.concatenate([density_ref[0, 0, at, :], density_ref[1, 0, at, :]], axis=1))
        left.append(kernels(slot, row))
    product = jnp.dot(
        jnp.concatenate(left, axis=1),
        jnp.concatenate(right, axis=0),
        preferred_element_type=jnp.float32,
    )
    width = product.shape[1] // 2
    real_part = product[:TILE, :width] - product[TILE:, width:]
    imag_part = product[:TILE, width:] + product[TILE:, :width]
    return real_part, imag_part


class Steps:
    def __init__(self, starts, offsets, sizes):
        self.starts, self.offsets, self.sizes = starts, offsets, sizes
        self.bounds = [sum(sizes[:at]) for at in range(len(sizes) + 1)]

    def part(self, step):
        return sum((step >= bound).astype(jnp.int32) for bound in self.bounds[1:-1])

    def mode(self, step):
        found = step - self.bounds[0] + self.starts[0] + self.offsets[0]
        for at in range(1, len(self.sizes)):
            here = step - self.bounds[at] + self.starts[at] + self.offsets[at]
            found = jnp.where(step >= self.bounds[at], here, found)
        return found

    def within(self, at, step):
        return jnp.clip(step - self.bounds[at], 0, self.sizes[at] - 1)

    def whole_spec(self, points, rhs, first=0):
        return pl.BlockSpec((2, 1, points, rhs), lambda i, *_: (0, self.mode(i) - first, 0, 0))

    def piece_spec(self, at, points, rhs, offset=0):
        return pl.BlockSpec((2, 1, points, rhs), lambda i, *_: (0, offset + self.within(at, i), 0, 0))


def partial_kernel(steps, index0, index1, index2, shard_ref, *refs):
    index_refs, kernel_refs, density_refs, out_refs = (index0, index1, index2), refs[:3], refs[3:15], refs[15:]
    step = pl.program_id(0)
    part = steps.part(step)
    first = steps.mode(step) * 16
    for at in range(3):

        @pl.when(part == at)
        def _(at=at):
            for row in range(2):
                sums = near_rows(
                    index_refs[at], shard_ref.at[pl.ds(4 * at, 4)], first, row,
                    lambda slot, row: kernel_refs[at][0, row, slot].reshape(2 * TILE, TILE),
                    density_refs[4 * at : 4 * at + 4],
                )
                for c in range(2):
                    out_refs[at][c, 0, pl.ds(row * TILE, TILE), :] = sums[c].astype(jnp.bfloat16)


def partial_near(steps, indexes, shard_ids, kernels, densities):
    rows, slots = kernels[0].shape[1:3]
    points, rhs = densities[0].shape[2:]
    count = sum(steps.sizes)
    return pl.pallas_call(
        functools.partial(partial_kernel, steps),
        grid_spec=pltpu.PrefetchScalarGridSpec(
            num_scalar_prefetch=4,
            grid=(count,),
            in_specs=[
                pl.BlockSpec((1, rows, slots, 2, TILE, TILE), lambda i, *_, at=at: (steps.within(at, i), 0, 0, 0, 0, 0))
                for at in range(3)
            ]
            + [steps.piece_spec(at, points, rhs, steps.offsets[at]) for at in range(3) for _ in range(4)],
            out_specs=[steps.piece_spec(at, points, rhs) for at in range(3)],
        ),
        out_shape=[jax.ShapeDtypeStruct((2, size, points, rhs), jnp.bfloat16) for size in steps.sizes],
        cost_estimate=pl.CostEstimate(flops=count * 540_000_000, bytes_accessed=count * 1_900_000, transcendentals=0),
        name="partial_near",
    )(*indexes, shard_ids, *kernels, *densities)


def own_kernel(steps, index_ref, shard_ref, *refs):
    kernel_refs, density_refs, own_ref, coupled_ref, out_ref = refs[:4], refs[4:16], refs[16], refs[17], refs[18]
    step = pl.program_id(0)
    part = steps.part(step)
    first = steps.mode(step) * 16
    for at in range(3):

        @pl.when(part == at)
        def _(at=at):
            for row in range(2):
                sums = near_rows(
                    index_ref, shard_ref.at[pl.ds(4 * at, 4)], first, row,
                    lambda slot, row: kernel_refs[slot][0, row, 0].reshape(2 * TILE, TILE),
                    density_refs[4 * at : 4 * at + 4],
                )
                rows = pl.ds(row * TILE, TILE)
                for c in range(2):
                    total = 0.5 * own_ref[c, 0, rows, :].astype(jnp.float32) + sums[c]
                    out_ref[c, 0, rows, :] = total + coupled_ref[c, 0, rows, :].astype(jnp.float32)


def own_near(steps, index, shard_ids, kernel_tiles, densities, density, coupled):
    rows = kernel_tiles.shape[1]
    points, rhs = density.shape[2:]
    count = sum(steps.sizes)

    def kernel_spec(slot):
        return pl.BlockSpec(
            (1, rows, 1, 2, TILE, TILE),
            lambda i, index_ref, shard_ref: (steps.mode(i), 0, shard_ref[4 * steps.part(i) + slot], 0, 0, 0),
        )

    return pl.pallas_call(
        functools.partial(own_kernel, steps),
        grid_spec=pltpu.PrefetchScalarGridSpec(
            num_scalar_prefetch=2,
            grid=(count,),
            in_specs=[kernel_spec(slot) for slot in range(4)]
            + [steps.piece_spec(at, points, rhs, steps.offsets[at]) for at in range(3) for _ in range(4)]
            + [steps.whole_spec(points, rhs)] * 2,
            out_specs=steps.whole_spec(points, rhs, steps.starts[0]),
        ),
        out_shape=jax.ShapeDtypeStruct((2, count, points, rhs), jnp.float32),
        cost_estimate=pl.CostEstimate(flops=count * 540_000_000, bytes_accessed=count * 2_600_000, transcendentals=0),
        name="own_near",
    )(index, shard_ids, *([kernel_tiles] * 4), *densities, density, coupled)


def final_kernel(places, base_ref, *refs):
    other_refs, out_ref = refs[: len(refs) - 8], refs[-7]
    base_buf, other_buf, out_buf, base_sem, other_sem, out_sem = refs[-6:]
    reads, writes = [], []
    for slot, (at, offset, inner, mode) in enumerate(places):
        reads.append(
            (
                pltpu.make_async_copy(base_ref.at[:, inner], base_buf.at[slot], base_sem.at[slot]),
                pltpu.make_async_copy(other_refs[at].at[:, offset], other_buf.at[slot], other_sem.at[slot]),
            )
        )
        writes.append(pltpu.make_async_copy(out_buf.at[slot], out_ref.at[:, mode], out_sem.at[slot]))
    for pair in reads:
        for copy in pair:
            copy.start()
    for slot, pair in enumerate(reads):
        for copy in pair:
            copy.wait()
        out_buf[slot] = (base_buf[slot] + other_buf[slot].astype(jnp.float32)).astype(out_buf.dtype)
        writes[slot].start()
    for copy in writes:
        copy.wait()


def final_sum(places, base, others, running):
    points, rhs = base.shape[2:]
    count = len(places)
    here = pl.BlockSpec(memory_space=pl.ANY)
    return pl.pallas_call(
        functools.partial(final_kernel, places),
        in_specs=[here] * (2 + len(others)),
        out_specs=here,
        out_shape=jax.ShapeDtypeStruct(running.shape, running.dtype),
        scratch_shapes=[
            pltpu.VMEM((count, 2, points, rhs), jnp.float32),
            pltpu.VMEM((count, 2, points, rhs), jnp.bfloat16),
            pltpu.VMEM((count, 2, points, rhs), jnp.bfloat16),
            pltpu.SemaphoreType.DMA((count,)),
            pltpu.SemaphoreType.DMA((count,)),
            pltpu.SemaphoreType.DMA((count,)),
        ],
        input_output_aliases={1 + len(others): 0},
        cost_estimate=pl.CostEstimate(flops=count * 262144, bytes_accessed=count * 1_050_000, transcendentals=0),
        name="final_sum",
    )(base, *others, running)


def pack_kernel(chunk_sizes, shard_ref, k0, k1, k2, k3, *out_refs):
    step = pl.program_id(0)
    bound = 0
    for size, out_ref in zip(chunk_sizes, out_refs, strict=True):

        @pl.when((step >= bound) & (step < bound + size))
        def _(out_ref=out_ref):
            for slot, kernel_ref in enumerate((k0, k1, k2, k3)):
                out_ref[:, :, slot] = kernel_ref[:, :, 0]

        bound += size


def pack(steps, chunk_sizes, shard_ids, kernel_tiles):
    rows = kernel_tiles.shape[1]
    count = sum(steps.sizes)

    def kernel_spec(slot):
        return pl.BlockSpec(
            (1, rows, 1, 2, TILE, TILE),
            lambda i, shard_ref: (steps.mode(i), 0, shard_ref[4 * lax.rem(steps.part(i), 3) + slot], 0, 0, 0),
        )

    def out_spec(bound, size):
        return pl.BlockSpec(
            (1, rows, 4, 2, TILE, TILE), lambda i, *_: (jnp.clip(i - bound, 0, size - 1), 0, 0, 0, 0, 0)
        )

    return pl.pallas_call(
        functools.partial(pack_kernel, chunk_sizes),
        grid_spec=pltpu.PrefetchScalarGridSpec(
            num_scalar_prefetch=1,
            grid=(count,),
            in_specs=[kernel_spec(slot) for slot in range(4)],
            out_specs=[out_spec(sum(chunk_sizes[:at]), size) for at, size in enumerate(chunk_sizes)],
        ),
        out_shape=[jax.ShapeDtypeStruct((size, rows, 4, 2, TILE, TILE), jnp.bfloat16) for size in chunk_sizes],
        cost_estimate=pl.CostEstimate(flops=0, bytes_accessed=count * 1_050_000, transcendentals=0),
        name="pack",
    )(shard_ids, *([kernel_tiles] * 4))


def couple_kernel(band, weight_ref, low_ref, own_ref, high_ref, out_ref):
    reach = band // 2
    modes = own_ref.shape[1]

    def window(c, mode):
        if mode < reach:
            return low_ref[c, mode].astype(jnp.float32)
        if mode < reach + modes:
            return own_ref[c, mode - reach].astype(jnp.float32)
        return high_ref[c, mode - reach - modes].astype(jnp.float32)

    shape = own_ref.shape[2:]
    for mode in range(modes):
        real_part = imag_part = None
        for offset in range(band):
            at = offset * modes + mode
            wr = jnp.broadcast_to(weight_ref[:, at : at + 1], shape)
            at += band * modes
            wi = jnp.broadcast_to(weight_ref[:, at : at + 1], shape)
            sr, si = window(0, mode + offset), window(1, mode + offset)
            real_now, imag_now = wr * sr - wi * si, wr * si + wi * sr
            real_part = real_now if real_part is None else real_part + real_now
            imag_part = imag_now if imag_part is None else imag_part + imag_now
        out_ref[0, mode] = real_part.astype(out_ref.dtype)
        out_ref[1, mode] = imag_part.astype(out_ref.dtype)


def couple(density, low, high, weights, rows=16):
    _, modes, points, rhs = density.shape
    band = weights.shape[1]
    reach = band // 2
    by_point = jnp.transpose(weights.astype(jnp.float32).reshape(2 * band * modes, points))

    def spec(count):
        return pl.BlockSpec((2, count, rows, rhs), lambda i: (0, 0, i, 0))

    return pl.pallas_call(
        functools.partial(couple_kernel, band),
        grid=(points // rows,),
        in_specs=[pl.BlockSpec((rows, by_point.shape[1]), lambda i: (i, 0)), spec(reach), spec(modes), spec(reach)],
        out_specs=spec(modes),
        out_shape=jax.ShapeDtypeStruct(density.shape, jnp.bfloat16),
        cost_estimate=pl.CostEstimate(flops=20_000_000_000, bytes_accessed=10_000_000, transcendentals=0),
        name="couple",
    )(by_point, low, density, high)


def apply(density, kernel_tiles, tile_index, coupling, spread, liner):
    band_count = coupling.shape[1]
    reach = band_count // 2
    mode_count = density.shape[1]
    node = node_of(lax.axis_index("blk"))
    sizes = [[sum(chunks) for chunks in group] for group in GROUPS]
    flat = [size for group in sizes for size in group]
    starts = [[sum(flat[: 3 * g + at]) for at in range(3)] for g in range(len(GROUPS))]
    masks = [[0, 1 << one, 1 << two, (1 << one) | (1 << two)] for one, two, _ in ROLES]
    held = jnp.stack([blk_of(node ^ mask) for some in masks for mask in some])
    theirs = jnp.stack(
        [blk_of(node ^ mask ^ (1 << role[2])) for role, some in zip(ROLES, masks, strict=True) for mask in some]
    )

    own, from_one, from_two, from_both = {}, {}, {}, {}
    for g in range(len(GROUPS)):
        for at, role in enumerate(ROLES):
            lo = starts[g][at]
            own[g, at] = lax.slice_in_dim(density, lo, lo + sizes[g][at], axis=1)
            from_one[g, at] = swap(own[g, at], role[0])
            from_two[g, at] = swap(own[g, at], role[1])
            from_both[g, at] = swap(from_one[g, at], role[1])
    devices = lax.axis_size("mode")
    forward = [(i, i + 1) for i in range(devices - 1)]
    backward = [(target, source) for source, target in forward]
    low = lax.ppermute(lax.slice_in_dim(density, mode_count - reach, None, axis=1), "mode", forward)
    high = lax.ppermute(lax.slice_in_dim(density, 0, reach, axis=1), "mode", backward)
    index = tile_index.reshape(-1)
    indexes = []
    for role in ROLES:
        indexes.append(swap(index, role[2]))

    chunks = [
        (g, [group[at][chunk] for at in range(3)], [sum(group[at][:chunk]) for at in range(3)])
        for g, group in reversed(tuple(enumerate(GROUPS)))
        for chunk in range(len(group[0]))
    ]
    packed = pack(
        Steps([start for group in starts for start in group], [0] * len(flat), flat),
        [size for group in GROUPS for some in group for size in some],
        theirs,
        kernel_tiles,
    )
    leaving, taken = {}, 0
    for g, group in enumerate(GROUPS):
        for at in range(3):
            for _ in group[at]:
                leaving.setdefault((g, at), []).append(packed[taken])
                taken += 1
    kernels = {}
    for c, (g, _, _) in enumerate(chunks):
        for at, role in enumerate(ROLES):
            kernels[c, at] = swap(leaving[g, at].pop(0), role[2])

    offsets = jnp.abs(jnp.arange(band_count, dtype=jnp.int32) - reach)
    within = (offsets[:, None] <= spread[None, :]) & (liner[None, :] == 1)
    weights = coupling * within[None, :, None, :].astype(jnp.bfloat16)
    coupled = couple(density, low, high, weights)
    densities = [
        [ref for at in range(3) for ref in (own[g, at], from_one[g, at], from_two[g, at], from_both[g, at])]
        for g in range(len(GROUPS))
    ]
    bases = []
    for g in range(len(GROUPS)):
        steps = Steps(starts[g], [0] * 3, sizes[g])
        bases.append(own_near(steps, index, held, kernel_tiles, densities[g], density, coupled))

    others = {}
    for c, (g, count, offset) in enumerate(chunks):
        sums = partial_near(
            Steps(starts[g], offset, count), indexes, held, [kernels[c, at] for at in range(3)], densities[g]
        )
        for at, role in enumerate(ROLES):
            others[c, at] = swap(sums[at], role[2])
    running = coupled
    for c, (g, count, offset) in enumerate(chunks):
        places = [
            (at, j, starts[g][at] + offset[at] + j - starts[g][0], starts[g][at] + offset[at] + j)
            for at in range(3)
            for j in range(count[at])
        ]
        running = final_sum(places, bases[g], [others[c, at] for at in range(3)], running)
    return running


def solution(mesh):
    return jax.shard_map(
        apply,
        mesh=mesh,
        in_specs=(
            P(None, "mode", "blk", None),
            P("mode", "blk", None, None, None, None),
            P("mode", "blk", None),
            P(None, None, "mode", "blk"),
            P("blk"),
            P("blk"),
        ),
        out_specs=P(None, "mode", "blk", None),
        check_vma=False,
    )
```

profile of v0, /device:TPU:0, one launch (start us, length us, event | category | flops | bytes accessed | tf_op | source)
XLA Modules:
  0.0 257.8 jit_solution(3869610814160902093)
XLA Ops:
  1.2 1.8 collective-permute-start
  3.0 2.2 collective-permute-start.1
  6.0 2.0 collective-permute-start.11
  9.7 2.3 collective-permute-start.3
  14.6 3.1 %collective-permute-start.2 = (bf16[2,1,256,256]{3,2,1,0:T(8,128)(2,1)S(1)}, bf16[2,1,256,256]{3,2,1,0:T(8,128)(2,1)S(1)}, u32[]{:S(2)}, u32[]{:S(2)}) collective-permute-start(bf16[2,1,256,256]{3,2,1,0:T(8,128)(2,1)S(1)} %collective-permute-done.refs_5_.refs_4_), channel_id=1, source_target_pairs={{0,96},{32,64},{96,0},{64,32},{16,112},{48,80},{112,16},{80,48},{1... | collective-permute-start | bytes 786440 | tf_op jit(solution)/shard_map/ppermute | solution.py:29
  18.3 13.9 %pack.1 = (bf16[1,2,4,2,128,128]{5,4,3,2,1,0:T(8,128)(2,1)}, bf16[1,2,4,2,128,128]{5,4,3,2,1,0:T(8,128)(2,1)}, bf16[1,2,4,2,128,128]{5,4,3,2,1,0:T(8,128)(2,1)},...) custom-call(s32[12]{0:T(128)} %stack.79.shard_ref, ...), custom_call_target="tpu_custom_call" | custom-call | bytes 16800000 | tf_op jit(solution)/shard_map/pack/pallas_call | solution.py:239
  37.4 3.9 %fusion = (bf16[2,4,256,256]{3,2,1,0:T(8,128)(2,1)S(1)}, bf16[2,4,256,256]{3,2,1,0:T(8,128)(2,1)S(1)}, bf16[2,4,256,256]{3,2,1,0:T(8,128)(2,1)}, bf16[2,4,256,256]{3,2,1,0:T(8,128)(2,1)}) fusion(bf16[2,16,256,256]{3,2,1,0:T(8,128)(2,1)} %refs_16_.3), kind=kLoop, calls=%fused_computation.5 | loop fusion | bytes 8388608 | tf_op jit(solution)/shard_map/slice | solution.py:318
  41.3 8.2 %collective-permute-done.5.refs_11_.refs_10_ = bf16[2,1,256,256]{3,2,1,0:T(8,128)(2,1)S(1)} collective-permute-done((bf16[2,1,256,256]{3,2,1,0:T(8,128)(2,1)S(1)}, bf16[2,1,256,256]{3,2,1,0:T(8,128)(2,1)S(1)}, u32[]{:S(2)}, u32[]{:S(2)}) %collective-permute-start.5) | collective-permute-done | bytes 262176 | tf_op jit(solution)/shard_map/ppermute | solution.py:29
  54.3 2.5 collective-permute-start.31
  58.1 5.5 %collective-permute-done.29.refs_0_ = bf16[1,2,4,2,128,128]{5,4,3,2,1,0:T(8,128)(2,1)S(1)} collective-permute-done((bf16[1,2,4,2,128,128]{5,4,3,2,1,0:T(8,128)(2,1)S(1)}, bf16[1,2,4,2,128,128]{5,4,3,2,1,0:T(8,128)(2,1)S(1)}, u32[]{:S(2)}, u32[]{:S(2)}) %collective-permute-start.29) | collective-permute-done | bytes 524320 | tf_op jit(solution)/shard_map/ppermute | solution.py:29
  63.7 2.5 collective-permute-start.26
  66.2 16.7 %collective-permute-done.30.refs_1_ = bf16[1,2,4,2,128,128]{5,4,3,2,1,0:T(8,128)(2,1)S(1)} collective-permute-done((bf16[1,2,4,2,128,128]{5,4,3,2,1,0:T(8,128)(2,1)S(1)}, bf16[1,2,4,2,128,128]{5,4,3,2,1,0:T(8,128)(2,1)S(1)}, u32[]{:S(2)}, u32[]{:S(2)}) %collective-permute-start.30) | collective-permute-done | bytes 524320 | tf_op jit(solution)/shard_map/ppermute | solution.py:29
  85.7 2.2 collective-permute-start.22
  87.9 22.2 %collective-permute-done.23.refs_9_.refs_8_ = bf16[2,4,256,256]{3,2,1,0:T(8,128)(2,1)S(1)} collective-permute-done((bf16[2,4,256,256]{3,2,1,0:T(8,128)(2,1)S(1)}, bf16[2,4,256,256]{3,2,1,0:T(8,128)(2,1)S(1)}, u32[]{:S(2)}, u32[]{:S(2)}) %collective-permute-start.23) | collective-permute-done | bytes 1048608 | tf_op jit(solution)/shard_map/ppermute | solution.py:29
  111.3 1.7 collective-permute-done.24.refs_10_.refs_9_
  118.0 14.6 %collective-permute-done.22.refs_7_.refs_6_ = bf16[2,4,256,256]{3,2,1,0:T(8,128)(2,1)S(1)} collective-permute-done((bf16[2,4,256,256]{3,2,1,0:T(8,128)(2,1)S(1)}, bf16[2,4,256,256]{3,2,1,0:T(8,128)(2,1)S(1)}, u32[]{:S(2)}, u32[]{:S(2)}) %collective-permute-start.22) | collective-permute-done | bytes 1048608 | tf_op jit(solution)/shard_map/ppermute | solution.py:29
  132.7 6.3 %collective-permute-done.25.refs_11_.refs_10_ = bf16[2,4,256,256]{3,2,1,0:T(8,128)(2,1)S(1)} collective-permute-done((bf16[2,4,256,256]{3,2,1,0:T(8,128)(2,1)S(1)}, bf16[2,4,256,256]{3,2,1,0:T(8,128)(2,1)S(1)}, u32[]{:S(2)}, u32[]{:S(2)}) %collective-permute-start.25) | collective-permute-done | bytes 1048608 | tf_op jit(solution)/shard_map/ppermute | solution.py:29
  139.1 2.3 collective-permute-start.9
  141.4 2.2 collective-permute-done.28.refs_15_.refs_14_
  147.0 1.9 copy.12
  149.5 5.4 %partial_near.3 = (bf16[2,1,256,256]{3,2,1,0:T(8,128)(2,1)}, bf16[2,1,256,256]{3,2,1,0:T(8,128)(2,1)}, bf16[2,1,256,256]{3,2,1,0:T(8,128)(2,1)}) custom-call(s32[256]{0:T(256)} %copy-done.35, s32[256]{0:T(256)} %collective-permute-done.12.index1, s32[256]{0:T(256)} %copy-done.36, s32[12]{0:T(128)} %stack.69.shard_ref, ...), custom_call_target="tpu_custom_call" | custom-call | flops 1620000000 | bytes 5700000 | tf_op jit(solution)/shard_map/partial_near/pallas_call | solution.py:98
  154.9 5.5 %partial_near.4 = (bf16[2,1,256,256]{3,2,1,0:T(8,128)(2,1)}, bf16[2,1,256,256]{3,2,1,0:T(8,128)(2,1)}, bf16[2,1,256,256]{3,2,1,0:T(8,128)(2,1)}) custom-call(s32[256]{0:T(256)} %copy-done.35, s32[256]{0:T(256)} %collective-permute-done.12.index1, s32[256]{0:T(256)} %copy-done.36, s32[12]{0:T(128)} %stack.69.shard_ref, ...), custom_call_target="tpu_custom_call" | custom-call | flops 1620000000 | bytes 5700000 | tf_op jit(solution)/shard_map/partial_near/pallas_call | solution.py:98
  160.4 20.7 %collective-permute-done.35.refs_0_ = bf16[3,2,4,2,128,128]{5,4,3,2,1,0:T(8,128)(2,1)} collective-permute-done((bf16[3,2,4,2,128,128]{5,4,3,2,1,0:T(8,128)(2,1)}, bf16[3,2,4,2,128,128]{5,4,3,2,1,0:T(8,128)(2,1)}, u32[]{:S(2)}, u32[]{:S(2)}) %collective-permute-start.35) | collective-permute-done | bytes 1572896 | tf_op jit(solution)/shard_map/ppermute | solution.py:29
  183.1 12.9 %partial_near.5 = (bf16[2,3,256,256]{3,2,1,0:T(8,128)(2,1)}, bf16[2,3,256,256]{3,2,1,0:T(8,128)(2,1)}, bf16[2,4,256,256]{3,2,1,0:T(8,128)(2,1)}) custom-call(s32[256]{0:T(256)} %copy-done.35, s32[256]{0:T(256)} %collective-permute-done.12.index1, s32[256]{0:T(256)} %copy-done.36, s32[12]{0:T(128)} %stack.69.shard_ref, ...), custom_call_target="tpu_custom_call" | custom-call | flops 5400000000 | bytes 19000000 | tf_op jit(solution)/shard_map/partial_near/pallas_call | solution.py:98
  196.0 1.7 collective-permute-start.38
  199.9 18.3 %couple.1.refs_17_.refs_3_ = bf16[2,16,256,256]{3,2,1,0:T(8,128)(2,1)} custom-call(f32[256,288]{1,0:T(8,128)} %bitcast.20, bf16[2,4,256,256]{3,2,1,0:T(8,128)(2,1)} %collective-permute-done.9.low_ref, bf16[2,16,256,256]{3,2,1,0:T(8,128)(2,1)} %refs_16_.3, bf16[2,4,256,256]{3,2,1,0:T(8,128)(2,1)} %collective-permute-done.10.high_ref), custom_call_target="tpu_custom_call" | custom-call | flops 20000000000 | bytes 10000000 | tf_op jit(solution)/shard_map/couple/pallas_call | solution.py:289
  218.2 6.2 %own_near.2.base_ref = f32[2,3,256,256]{3,2,1,0:T(8,128)} custom-call(s32[256]{0:T(256)} %copy-done.34, s32[12]{0:T(128)} %stack.69.shard_ref, bf16[16,2,8,2,128,128]{5,4,3,2,1,0:T(8,128)(2,1)} %refs_3_.3, bf16[16,2,8,2,128,128]{5,4,3,2,1,0:T(8,128)(2,1)} %refs_3_.3, bf16[16,2,8,2,128,128]{5,4,3,2,1,0:T(8,128)(2,1)} %refs_3_.3, ...), custom_call_target="tpu_custom_call" | custom-call | flops 1620000000 | bytes 7800000 | tf_op jit(solution)/shard_map/own_near/pallas_call | solution.py:148
  224.5 2.5 collective-permute-start.19
  229.1 17.4 %own_near.3.base_ref = f32[2,13,256,256]{3,2,1,0:T(8,128)} custom-call(s32[256]{0:T(256)} %copy-done.34, s32[12]{0:T(128)} %stack.69.shard_ref, bf16[16,2,8,2,128,128]{5,4,3,2,1,0:T(8,128)(2,1)} %refs_3_.3, bf16[16,2,8,2,128,128]{5,4,3,2,1,0:T(8,128)(2,1)} %refs_3_.3, bf16[16,2,8,2,128,128]{5,4,3,2,1,0:T(8,128)(2,1)} %refs_3_.3, ...), custom_call_target="tpu_custom_call" | custom-call | flops 7020000256 | bytes 33800000 | tf_op jit(solution)/shard_map/own_near/pallas_call | solution.py:148
  246.6 4.8 %final_sum.3.refs_3_ = bf16[2,16,256,256]{3,2,1,0:T(8,128)(2,1)} custom-call(f32[2,13,256,256]{3,2,1,0:T(8,128)} %own_near.3.base_ref, bf16[2,3,256,256]{3,2,1,0:T(8,128)(2,1)} %copy-done.16, bf16[2,3,256,256]{3,2,1,0:T(8,128)(2,1)} %copy-done.17, bf16[2,4,256,256]{3,2,1,0:T(8,128)(2,1)} %copy-done.15, ...), custom_call_target="tpu_custom_call", output_to_operand_aliasing={{}: (4, {})} | custom-call | flops 2621440 | bytes 10500000 | tf_op jit(solution)/shard_map/final_sum/pallas_call | solution.py:192
  252.8 2.4 final_sum.4.refs_3_
  255.3 2.4 final_sum.5
  (163 shorter events, 38.9 us)
Async XLA Ops:
  9.7 22.6 %collective-permute-start.3 = (bf16[2,1,256,256]{3,2,1,0:T(8,128)(2,1)S(1)}, bf16[2,1,256,256]{3,2,1,0:T(8,128)(2,1)S(1)}, u32[]{:S(2)}, u32[]{:S(2)}) collective-permute-start(bf16[2,1,256,256]{3,2,1,0:T(8,128)(2,1)S(1)} %get-tuple-element.46.refs_8_.refs_7_), channel_id=1, source_target_pairs={{0,96},{32,64},{96,0},{64,32},{16,112},{48,80},{112,16},{80,48},{1... | collective-permute-start | bytes 786440 | tf_op jit(solution)/shard_map/ppermute | solution.py:29
  12.0 20.8 %collective-permute-start.4 = (bf16[2,1,256,256]{3,2,1,0:T(8,128)(2,1)S(1)}, bf16[2,1,256,256]{3,2,1,0:T(8,128)(2,1)S(1)}, u32[]{:S(2)}, u32[]{:S(2)}) collective-permute-start(bf16[2,1,256,256]{3,2,1,0:T(8,128)(2,1)S(1)} %get-tuple-element.46.refs_8_.refs_7_), channel_id=1, source_target_pairs={{0,16},{32,48},{96,112},{64,80},{16,0},{48,32},{112,96},{80,64},{1... | collective-permute-start | bytes 786440 | tf_op jit(solution)/shard_map/ppermute | solution.py:29
  13.5 20.4 %collective-permute-start.6 = (bf16[2,1,256,256]{3,2,1,0:T(8,128)(2,1)S(1)}, bf16[2,1,256,256]{3,2,1,0:T(8,128)(2,1)S(1)}, u32[]{:S(2)}, u32[]{:S(2)}) collective-permute-start(bf16[2,1,256,256]{3,2,1,0:T(8,128)(2,1)S(1)} %get-tuple-element.45.refs_12_.refs_11_), channel_id=1, source_target_pairs={{0,16},{32,48},{96,112},{64,80},{16,0},{48,32},{112,96},{80,64},{1... | collective-permute-start | bytes 786440 | tf_op jit(solution)/shard_map/ppermute | solution.py:29
  14.0 21.0 %collective-permute-start.7 = (bf16[2,1,256,256]{3,2,1,0:T(8,128)(2,1)S(1)}, bf16[2,1,256,256]{3,2,1,0:T(8,128)(2,1)S(1)}, u32[]{:S(2)}, u32[]{:S(2)}) collective-permute-start(bf16[2,1,256,256]{3,2,1,0:T(8,128)(2,1)S(1)} %get-tuple-element.45.refs_12_.refs_11_), channel_id=1, source_target_pairs={{0,32},{32,0},{96,64},{64,96},{16,48},{48,16},{112,80},{80,112},{1... | collective-permute-start | bytes 786440 | tf_op jit(solution)/shard_map/ppermute | solution.py:29
  14.6 21.7 %collective-permute-start.2 = (bf16[2,1,256,256]{3,2,1,0:T(8,128)(2,1)S(1)}, bf16[2,1,256,256]{3,2,1,0:T(8,128)(2,1)S(1)}, u32[]{:S(2)}, u32[]{:S(2)}) collective-permute-start(bf16[2,1,256,256]{3,2,1,0:T(8,128)(2,1)S(1)} %collective-permute-done.refs_5_.refs_4_), channel_id=1, source_target_pairs={{0,96},{32,64},{96,0},{64,32},{16,112},{48,80},{112,16},{80,48},{1... | collective-permute-start | bytes 786440 | tf_op jit(solution)/shard_map/ppermute | solution.py:29
  32.3 20.5 %collective-permute-start.14 = (bf16[1,2,4,2,128,128]{5,4,3,2,1,0:T(8,128)(2,1)}, bf16[1,2,4,2,128,128]{5,4,3,2,1,0:T(8,128)(2,1)S(1)}, u32[]{:S(2)}, u32[]{:S(2)}) collective-permute-start(bf16[1,2,4,2,128,128]{5,4,3,2,1,0:T(8,128)(2,1)} %get-tuple-element.23), channel_id=1, source_target_pairs={{0,16},{32,48},{96,112},{64,80},{16,0},{48,32},{112,96},{80,64},{1... | collective-permute-start | bytes 1572872 | tf_op jit(solution)/shard_map/ppermute | solution.py:29
  32.8 20.7 %collective-permute-start.15 = (bf16[1,2,4,2,128,128]{5,4,3,2,1,0:T(8,128)(2,1)}, bf16[1,2,4,2,128,128]{5,4,3,2,1,0:T(8,128)(2,1)S(1)}, u32[]{:S(2)}, u32[]{:S(2)}) collective-permute-start(bf16[1,2,4,2,128,128]{5,4,3,2,1,0:T(8,128)(2,1)} %get-tuple-element.24), channel_id=1, source_target_pairs={{0,32},{32,0},{96,64},{64,96},{16,48},{48,16},{112,80},{80,112},{1... | collective-permute-start | bytes 1572872 | tf_op jit(solution)/shard_map/ppermute | solution.py:29
  49.5 35.0 %collective-permute-start.20 = (bf16[2,4,256,256]{3,2,1,0:T(8,128)(2,1)S(1)}, bf16[2,4,256,256]{3,2,1,0:T(8,128)(2,1)S(1)}, u32[]{:S(2)}, u32[]{:S(2)}) collective-permute-start(bf16[2,4,256,256]{3,2,1,0:T(8,128)(2,1)S(1)} %get-tuple-element.42.refs_4_.refs_3_), channel_id=1, source_target_pairs={{0,32},{32,0},{96,64},{64,96},{16,48},{48,16},{112,80},{80,112},{1... | collective-permute-start | bytes 3145736 | tf_op jit(solution)/shard_map/ppermute | solution.py:29
  52.8 32.9 %collective-permute-start.21 = (bf16[2,4,256,256]{3,2,1,0:T(8,128)(2,1)S(1)}, bf16[2,4,256,256]{3,2,1,0:T(8,128)(2,1)S(1)}, u32[]{:S(2)}, u32[]{:S(2)}) collective-permute-start(bf16[2,4,256,256]{3,2,1,0:T(8,128)(2,1)S(1)} %get-tuple-element.42.refs_4_.refs_3_), channel_id=1, source_target_pairs={{0,96},{32,64},{96,0},{64,32},{16,112},{48,80},{112,16},{80,48},{1... | collective-permute-start | bytes 3145736 | tf_op jit(solution)/shard_map/ppermute | solution.py:29
  53.5 29.4 %collective-permute-start.30 = (bf16[1,2,4,2,128,128]{5,4,3,2,1,0:T(8,128)(2,1)S(1)}, bf16[1,2,4,2,128,128]{5,4,3,2,1,0:T(8,128)(2,1)S(1)}, u32[]{:S(2)}, u32[]{:S(2)}) collective-permute-start(bf16[1,2,4,2,128,128]{5,4,3,2,1,0:T(8,128)(2,1)S(1)} %copy-done.42), channel_id=1, source_target_pairs={{0,32},{32,0},{96,64},{64,96},{16,48},{48,16},{112,80},{80,112},{1... | collective-permute-start | bytes 1572872 | tf_op jit(solution)/shard_map/ppermute | solution.py:29
  54.3 30.0 %collective-permute-start.31 = (bf16[1,2,4,2,128,128]{5,4,3,2,1,0:T(8,128)(2,1)S(1)}, bf16[1,2,4,2,128,128]{5,4,3,2,1,0:T(8,128)(2,1)S(1)}, u32[]{:S(2)}, u32[]{:S(2)}) collective-permute-start(bf16[1,2,4,2,128,128]{5,4,3,2,1,0:T(8,128)(2,1)S(1)} %copy-done.41), channel_id=1, source_target_pairs={{0,96},{32,64},{96,0},{64,32},{16,112},{48,80},{112,16},{80,48},{1... | collective-permute-start | bytes 1572872 | tf_op jit(solution)/shard_map/ppermute | solution.py:29
  63.7 47.6 %collective-permute-start.26 = (bf16[2,5,256,256]{3,2,1,0:T(8,128)(2,1)S(1)}, bf16[2,5,256,256]{3,2,1,0:T(8,128)(2,1)S(1)}, u32[]{:S(2)}, u32[]{:S(2)}) collective-permute-start(bf16[2,5,256,256]{3,2,1,0:T(8,128)(2,1)S(1)} %slice.31.refs_12_.refs_11_), channel_id=1, source_target_pairs={{0,16},{32,48},{96,112},{64,80},{16,0},{48,32},{112,96},{80,64},{1... | collective-permute-start | bytes 3932168 | tf_op jit(solution)/shard_map/ppermute | solution.py:29
  82.9 27.2 %collective-permute-start.23 = (bf16[2,4,256,256]{3,2,1,0:T(8,128)(2,1)S(1)}, bf16[2,4,256,256]{3,2,1,0:T(8,128)(2,1)S(1)}, u32[]{:S(2)}, u32[]{:S(2)}) collective-permute-start(bf16[2,4,256,256]{3,2,1,0:T(8,128)(2,1)S(1)} %get-tuple-element.41.refs_8_.refs_7_), channel_id=1, source_target_pairs={{0,96},{32,64},{96,0},{64,32},{16,112},{48,80},{112,16},{80,48},{1... | collective-permute-start | bytes 3145736 | tf_op jit(solution)/shard_map/ppermute | solution.py:29
  84.3 31.2 %collective-permute-start.27 = (bf16[2,5,256,256]{3,2,1,0:T(8,128)(2,1)S(1)}, bf16[2,5,256,256]{3,2,1,0:T(8,128)(2,1)S(1)}, u32[]{:S(2)}, u32[]{:S(2)}) collective-permute-start(bf16[2,5,256,256]{3,2,1,0:T(8,128)(2,1)S(1)} %slice.31.refs_12_.refs_11_), channel_id=1, source_target_pairs={{0,32},{32,0},{96,64},{64,96},{16,48},{48,16},{112,80},{80,112},{1... | collective-permute-start | bytes 3932168 | tf_op jit(solution)/shard_map/ppermute | solution.py:29
  84.5 28.6 %collective-permute-start.24 = (bf16[2,4,256,256]{3,2,1,0:T(8,128)(2,1)S(1)}, bf16[2,4,256,256]{3,2,1,0:T(8,128)(2,1)S(1)}, u32[]{:S(2)}, u32[]{:S(2)}) collective-permute-start(bf16[2,4,256,256]{3,2,1,0:T(8,128)(2,1)S(1)} %get-tuple-element.41.refs_8_.refs_7_), channel_id=1, source_target_pairs={{0,16},{32,48},{96,112},{64,80},{16,0},{48,32},{112,96},{80,64},{1... | collective-permute-start | bytes 3145736 | tf_op jit(solution)/shard_map/ppermute | solution.py:29
  85.7 46.9 %collective-permute-start.22 = (bf16[2,4,256,256]{3,2,1,0:T(8,128)(2,1)S(1)}, bf16[2,4,256,256]{3,2,1,0:T(8,128)(2,1)S(1)}, u32[]{:S(2)}, u32[]{:S(2)}) collective-permute-start(bf16[2,4,256,256]{3,2,1,0:T(8,128)(2,1)S(1)} %collective-permute-done.20.refs_5_.refs_4_), channel_id=1, source_target_pairs={{0,96},{32,64},{96,0},{64,32},{16,112},{48,80},{112,16},{80,48},{1... | collective-permute-start | bytes 3145736 | tf_op jit(solution)/shard_map/ppermute | solution.py:29
  110.1 73.0 %collective-permute-start.37 = (bf16[4,2,4,2,128,128]{5,4,3,2,1,0:T(8,128)(2,1)}, bf16[4,2,4,2,128,128]{5,4,3,2,1,0:T(8,128)(2,1)}, u32[]{:S(2)}, u32[]{:S(2)}) collective-permute-start(bf16[4,2,4,2,128,128]{5,4,3,2,1,0:T(8,128)(2,1)} %get-tuple-element.37), channel_id=1, source_target_pairs={{0,96},{32,64},{96,0},{64,32},{16,112},{48,80},{112,16},{80,48},{1... | collective-permute-start | bytes 6291464 | tf_op jit(solution)/shard_map/ppermute | solution.py:29
  111.3 32.3 %collective-permute-start.28 = (bf16[2,5,256,256]{3,2,1,0:T(8,128)(2,1)S(1)}, bf16[2,5,256,256]{3,2,1,0:T(8,128)(2,1)S(1)}, u32[]{:S(2)}, u32[]{:S(2)}) collective-permute-start(bf16[2,5,256,256]{3,2,1,0:T(8,128)(2,1)S(1)} %collective-permute-done.26.refs_13_.refs_12_), channel_id=1, source_target_pairs={{0,32},{32,0},{96,64},{64,96},{16,48},{48,16},{112,80},{80,112},{1... | collective-permute-start | bytes 3932168 | tf_op jit(solution)/shard_map/ppermute | solution.py:29
  113.0 26.0 %collective-permute-start.25 = (bf16[2,4,256,256]{3,2,1,0:T(8,128)(2,1)S(1)}, bf16[2,4,256,256]{3,2,1,0:T(8,128)(2,1)S(1)}, u32[]{:S(2)}, u32[]{:S(2)}) collective-permute-start(bf16[2,4,256,256]{3,2,1,0:T(8,128)(2,1)S(1)} %collective-permute-done.23.refs_9_.refs_8_), channel_id=1, source_target_pairs={{0,16},{32,48},{96,112},{64,80},{16,0},{48,32},{112,96},{80,64},{1... | collective-permute-start | bytes 3145736 | tf_op jit(solution)/shard_map/ppermute | solution.py:29
  116.6 64.5 %collective-permute-start.35 = (bf16[3,2,4,2,128,128]{5,4,3,2,1,0:T(8,128)(2,1)}, bf16[3,2,4,2,128,128]{5,4,3,2,1,0:T(8,128)(2,1)}, u32[]{:S(2)}, u32[]{:S(2)}) collective-permute-start(bf16[3,2,4,2,128,128]{5,4,3,2,1,0:T(8,128)(2,1)} %get-tuple-element.35), channel_id=1, source_target_pairs={{0,16},{32,48},{96,112},{64,80},{16,0},{48,32},{112,96},{80,64},{1... | collective-permute-start | bytes 4718600 | tf_op jit(solution)/shard_map/ppermute | solution.py:29
  132.6 50.2 %collective-permute-start.36 = (bf16[3,2,4,2,128,128]{5,4,3,2,1,0:T(8,128)(2,1)}, bf16[3,2,4,2,128,128]{5,4,3,2,1,0:T(8,128)(2,1)}, u32[]{:S(2)}, u32[]{:S(2)}) collective-permute-start(bf16[3,2,4,2,128,128]{5,4,3,2,1,0:T(8,128)(2,1)} %get-tuple-element.36), channel_id=1, source_target_pairs={{0,32},{32,0},{96,64},{64,96},{16,48},{48,16},{112,80},{80,112},{1... | collective-permute-start | bytes 4718600 | tf_op jit(solution)/shard_map/ppermute | solution.py:29
  139.1 58.7 %collective-permute-start.9 = (bf16[2,4,256,256]{3,2,1,0:T(8,128)(2,1)}, bf16[2,4,256,256]{3,2,1,0:T(8,128)(2,1)}, u32[]{:S(2)}, u32[]{:S(2)}) collective-permute-start(bf16[2,4,256,256]{3,2,1,0:T(8,128)(2,1)} %get-tuple-element.44), channel_id=1, source_target_pairs={{0,1},{1,2},{2,3},{3,4},{4,5},{5,6},{6,7},{7,8},{8,9},{9,10},{10,1... | collective-permute-start | bytes 3145736 | tf_op jit(solution)/shard_map/ppermute | solution.py:325
  144.6 53.8 %collective-permute-start.10 = (bf16[2,4,256,256]{3,2,1,0:T(8,128)(2,1)}, bf16[2,4,256,256]{3,2,1,0:T(8,128)(2,1)}, u32[]{:S(2)}, u32[]{:S(2)}) collective-permute-start(bf16[2,4,256,256]{3,2,1,0:T(8,128)(2,1)} %get-tuple-element.43), channel_id=1, source_target_pairs={{1,0},{2,1},{3,2},{4,3},{5,4},{6,5},{7,6},{8,7},{9,8},{10,9},{11,1... | collective-permute-start | bytes 3145736 | tf_op jit(solution)/shard_map/ppermute | solution.py:326
  181.1 74.2 %collective-permute-start.17 = (bf16[2,1,256,256]{3,2,1,0:T(8,128)(2,1)}, bf16[2,1,256,256]{3,2,1,0:T(8,128)(2,1)}, u32[]{:S(2)}, u32[]{:S(2)}) collective-permute-start(bf16[2,1,256,256]{3,2,1,0:T(8,128)(2,1)} %get-tuple-element.26), channel_id=1, source_target_pairs={{0,16},{32,48},{96,112},{64,80},{16,0},{48,32},{112,96},{80,64},{1... | collective-permute-start | bytes 786440 | tf_op jit(solution)/shard_map/ppermute | solution.py:29
  182.8 41.6 %collective-permute-start.32 = (bf16[2,1,256,256]{3,2,1,0:T(8,128)(2,1)}, bf16[2,1,256,256]{3,2,1,0:T(8,128)(2,1)S(1)}, u32[]{:S(2)}, u32[]{:S(2)}) collective-permute-start(bf16[2,1,256,256]{3,2,1,0:T(8,128)(2,1)} %get-tuple-element.32), channel_id=1, source_target_pairs={{0,16},{32,48},{96,112},{64,80},{16,0},{48,32},{112,96},{80,64},{1... | collective-permute-start | bytes 786440 | tf_op jit(solution)/shard_map/ppermute | solution.py:29
  196.0 28.5 %collective-permute-start.38 = (bf16[2,3,256,256]{3,2,1,0:T(8,128)(2,1)}, bf16[2,3,256,256]{3,2,1,0:T(8,128)(2,1)S(1)}, u32[]{:S(2)}, u32[]{:S(2)}) collective-permute-start(bf16[2,3,256,256]{3,2,1,0:T(8,128)(2,1)} %get-tuple-element.38), channel_id=1, source_target_pairs={{0,16},{32,48},{96,112},{64,80},{16,0},{48,32},{112,96},{80,64},{1... | collective-permute-start | bytes 2359304 | tf_op jit(solution)/shard_map/ppermute | solution.py:29
  197.8 29.3 %collective-permute-start.39 = (bf16[2,3,256,256]{3,2,1,0:T(8,128)(2,1)}, bf16[2,3,256,256]{3,2,1,0:T(8,128)(2,1)S(1)}, u32[]{:S(2)}, u32[]{:S(2)}) collective-permute-start(bf16[2,3,256,256]{3,2,1,0:T(8,128)(2,1)} %get-tuple-element.39), channel_id=1, source_target_pairs={{0,32},{32,0},{96,64},{64,96},{16,48},{48,16},{112,80},{80,112},{1... | collective-permute-start | bytes 2359304 | tf_op jit(solution)/shard_map/ppermute | solution.py:29
  198.4 29.3 %collective-permute-start.40 = (bf16[2,4,256,256]{3,2,1,0:T(8,128)(2,1)}, bf16[2,4,256,256]{3,2,1,0:T(8,128)(2,1)S(1)}, u32[]{:S(2)}, u32[]{:S(2)}) collective-permute-start(bf16[2,4,256,256]{3,2,1,0:T(8,128)(2,1)} %get-tuple-element.40), channel_id=1, source_target_pairs={{0,96},{32,64},{96,0},{64,32},{16,112},{48,80},{112,16},{80,48},{1... | collective-permute-start | bytes 3145736 | tf_op jit(solution)/shard_map/ppermute | solution.py:29
  224.4 30.9 %collective-permute-start.18 = (bf16[2,1,256,256]{3,2,1,0:T(8,128)(2,1)}, bf16[2,1,256,256]{3,2,1,0:T(8,128)(2,1)}, u32[]{:S(2)}, u32[]{:S(2)}) collective-permute-start(bf16[2,1,256,256]{3,2,1,0:T(8,128)(2,1)} %get-tuple-element.27), channel_id=1, source_target_pairs={{0,32},{32,0},{96,64},{64,96},{16,48},{48,16},{112,80},{80,112},{1... | collective-permute-start | bytes 786440 | tf_op jit(solution)/shard_map/ppermute | solution.py:29
  224.5 30.8 %collective-permute-start.19 = (bf16[2,1,256,256]{3,2,1,0:T(8,128)(2,1)}, bf16[2,1,256,256]{3,2,1,0:T(8,128)(2,1)}, u32[]{:S(2)}, u32[]{:S(2)}) collective-permute-start(bf16[2,1,256,256]{3,2,1,0:T(8,128)(2,1)} %get-tuple-element.28), channel_id=1, source_target_pairs={{0,96},{32,64},{96,0},{64,32},{16,112},{48,80},{112,16},{80,48},{1... | collective-permute-start | bytes 786440 | tf_op jit(solution)/shard_map/ppermute | solution.py:29
  227.0 24.4 %collective-permute-start.33 = (bf16[2,1,256,256]{3,2,1,0:T(8,128)(2,1)}, bf16[2,1,256,256]{3,2,1,0:T(8,128)(2,1)S(1)}, u32[]{:S(2)}, u32[]{:S(2)}) collective-permute-start(bf16[2,1,256,256]{3,2,1,0:T(8,128)(2,1)} %get-tuple-element.33), channel_id=1, source_target_pairs={{0,32},{32,0},{96,64},{64,96},{16,48},{48,16},{112,80},{80,112},{1... | collective-permute-start | bytes 786440 | tf_op jit(solution)/shard_map/ppermute | solution.py:29
  227.7 23.8 %collective-permute-start.34 = (bf16[2,1,256,256]{3,2,1,0:T(8,128)(2,1)}, bf16[2,1,256,256]{3,2,1,0:T(8,128)(2,1)S(1)}, u32[]{:S(2)}, u32[]{:S(2)}) collective-permute-start(bf16[2,1,256,256]{3,2,1,0:T(8,128)(2,1)} %get-tuple-element.34), channel_id=1, source_target_pairs={{0,96},{32,64},{96,0},{64,32},{16,112},{48,80},{112,16},{80,48},{1... | collective-permute-start | bytes 786440 | tf_op jit(solution)/shard_map/ppermute | solution.py:29
  (54 other events, 1837.4 us)
where the time goes:
time: 259 us; the launch traced here: 258 us
  waiting for transfers between devices  101 us (39%)
  Pallas kernels  89.2 us (34%)
  starting transfers between devices  51.1 us (20%)
  local copies, waits for them, and re-layouts  14.8 us (6%)
    ppermute x39, waiting for transfers between devices, swap(): return lax.ppermute(block, 'blk', pairs)  101 us
    ppermute x39, starting transfers between devices, swap(): return lax.ppermute(block, 'blk', pairs)  47.3 us
    pallas_call x3, Pallas kernels, partial_near(): pl.pallas_call(functools.partial(partial_kernel, steps), grid_spec=pltpu....  23.8 us
    pallas_call x2, Pallas kernels, own_near(): pl.pallas_call(functools.partial(own_kernel, steps), grid_spec=pltpu.Pref...  23.6 us
    pallas_call x1, Pallas kernels, couple(): pl.pallas_call(functools.partial(couple_kernel, band), grid=(points // ro...  18.3 us
    pallas_call x1, Pallas kernels, pack(): pl.pallas_call(functools.partial(pack_kernel, chunk_sizes), grid_spec=plt...  13.9 us
    pallas_call x3, Pallas kernels, final_sum(): pl.pallas_call(functools.partial(final_kernel, places), in_specs=[here] *...  9.6 us
    slice x3, local copies, waits for them, and re-layouts, apply(): own[g, at] = lax.slice_in_dim(density, lo, lo + sizes[g][at], axis=1)  6.42 us
  transfers between devices with their start and end apart: 41, of which 14 were waited for; matrix products, arithmetic and copies ran while one was open for 4% of the time, Pallas kernels for 34%

commit v1 on v0

--- a/solution.py
+++ b/solution.py
@@ -11,7 +11,7 @@
 TILE = 128
 ROLES = ((0, 1, 2), (1, 2, 0), (2, 0, 1))
 
-GROUPS = (((1,), (1,), (1,)), ((3, 1), (3, 1), (4, 1)))
+GROUPS = (((1,), (1,), (1,)), ((2, 2), (2, 2), (3, 2)))
 
 
 def blk_of(node):
@@ -165,21 +165,24 @@
     other_refs, out_ref = refs[: len(refs) - 8], refs[-7]
     base_buf, other_buf, out_buf, base_sem, other_sem, out_sem = refs[-6:]
     reads, writes = [], []
-    for slot, (at, offset, inner, mode) in enumerate(places):
+    for slot, (at, offset, inner, mode) in enumerate(place for place in places for _ in range(2)):
+        place, c = slot // 2, slot % 2
         reads.append(
             (
-                pltpu.make_async_copy(base_ref.at[:, inner], base_buf.at[slot], base_sem.at[slot]),
-                pltpu.make_async_copy(other_refs[at].at[:, offset], other_buf.at[slot], other_sem.at[slot]),
+                pltpu.make_async_copy(base_ref.at[c, inner], base_buf.at[place, c], base_sem.at[slot]),
+                pltpu.make_async_copy(other_refs[at].at[c, offset], other_buf.at[place, c], other_sem.at[slot]),
             )
         )
-        writes.append(pltpu.make_async_copy(out_buf.at[slot], out_ref.at[:, mode], out_sem.at[slot]))
+        writes.append(pltpu.make_async_copy(out_buf.at[place, c], out_ref.at[c, mode], out_sem.at[slot]))
     for pair in reads:
         for copy in pair:
             copy.start()
     for slot, pair in enumerate(reads):
         for copy in pair:
             copy.wait()
-        out_buf[slot] = (base_buf[slot] + other_buf[slot].astype(jnp.float32)).astype(out_buf.dtype)
+        place, c = slot // 2, slot % 2
+        total = base_buf[place, c] + other_buf[place, c].astype(jnp.float32)
+        out_buf[place, c] = total.astype(out_buf.dtype)
         writes[slot].start()
     for copy in writes:
         copy.wait()
@@ -198,9 +201,9 @@
             pltpu.VMEM((count, 2, points, rhs), jnp.float32),
             pltpu.VMEM((count, 2, points, rhs), jnp.bfloat16),
             pltpu.VMEM((count, 2, points, rhs), jnp.bfloat16),
-            pltpu.SemaphoreType.DMA((count,)),
-            pltpu.SemaphoreType.DMA((count,)),
-            pltpu.SemaphoreType.DMA((count,)),
+            pltpu.SemaphoreType.DMA((2 * count,)),
+            pltpu.SemaphoreType.DMA((2 * count,)),
+            pltpu.SemaphoreType.DMA((2 * count,)),
         ],
         input_output_aliases={1 + len(others): 0},
         cost_estimate=pl.CostEstimate(flops=count * 262144, bytes_accessed=count * 1_050_000, transcendentals=0),

time: 259 us -> 276 us (1.066)
  the two profiles are of different devices: /device:TPU:0 before, /device:TPU:1 now
where the time goes in v1:
time: 276 us; the launch traced here: 273 us
  waiting for transfers between devices  104 us (38%)
  Pallas kernels  90.9 us (33%)
  starting transfers between devices  62.3 us (23%)
  local copies, waits for them, and re-layouts  13.9 us (5%)
    ppermute x39, waiting for transfers between devices, swap(): return lax.ppermute(block, 'blk', pairs)  104 us
    ppermute x39, starting transfers between devices, swap(): return lax.ppermute(block, 'blk', pairs)  36.1 us
    pallas_call x3, Pallas kernels, partial_near(): pl.pallas_call(functools.partial(partial_kernel, steps), grid_spec=pltpu....  24 us
    pallas_call x2, Pallas kernels, own_near(): pl.pallas_call(functools.partial(own_kernel, steps), grid_spec=pltpu.Pref...  23.6 us
    pallas_call x1, Pallas kernels, couple(): pl.pallas_call(functools.partial(couple_kernel, band), grid=(points // ro...  18.3 us
    pallas_call x1, Pallas kernels, pack(): pl.pallas_call(functools.partial(pack_kernel, chunk_sizes), grid_spec=plt...  15 us
    ppermute x1, starting transfers between devices, apply(): lax.ppermute(lax.slice_in_dim(density, mode_count - reach, None, axis=1),...  14.9 us
    ppermute x1, starting transfers between devices, apply(): lax.ppermute(lax.slice_in_dim(density, 0, reach, axis=1), 'mode', backward)  11.4 us
  transfers between devices with their start and end apart: 41, of which 11 were waited for; matrix products, arithmetic and copies ran while one was open for 4% of the time, Pallas kernels for 32%

profile of v1, /device:TPU:1, one launch (start us, length us, event | category | flops | bytes accessed | tf_op | source)
XLA Modules:
  0.0 273.1 jit_solution(14780360759847007435)
XLA Ops:
  1.2 2.2 collective-permute-start
  3.4 1.9 collective-permute-start.1
  6.1 1.6 collective-permute-start.6
  8.7 4.2 %collective-permute-done.11.index0 = s32[256]{0:T(256)S(1)} collective-permute-done((s32[256]{0:T(256)S(1)}, s32[256]{0:T(256)S(1)}, u32[]{:S(2)}, u32[]{:S(2)}) %collective-permute-start.11) | collective-permute-done | bytes 1056 | tf_op jit(solution)/shard_map/ppermute | solution.py:29
  12.9 2.8 %collective-permute-done.12.index1 = s32[256]{0:T(256)S(1)} collective-permute-done((s32[256]{0:T(256)S(1)}, s32[256]{0:T(256)S(1)}, u32[]{:S(2)}, u32[]{:S(2)}) %collective-permute-start.12) | collective-permute-done | bytes 1056 | tf_op jit(solution)/shard_map/ppermute | solution.py:29
  15.7 1.9 collective-permute-start.13
  17.6 1.7 collective-permute-done.13.index2
  20.7 2.0 collective-permute-start.2
  23.7 3.9 %fusion = (bf16[2,4,256,256]{3,2,1,0:T(8,128)(2,1)S(1)}, bf16[2,4,256,256]{3,2,1,0:T(8,128)(2,1)S(1)}, bf16[2,4,256,256]{3,2,1,0:T(8,128)(2,1)}, bf16[2,4,256,256]{3,2,1,0:T(8,128)(2,1)}) fusion(bf16[2,16,256,256]{3,2,1,0:T(8,128)(2,1)} %refs_16_.3), kind=kLoop, calls=%fused_computation.5 | loop fusion | bytes 8388608 | tf_op jit(solution)/shard_map/slice | solution.py:321
  29.8 15.0 %pack.1 = (bf16[1,2,4,2,128,128]{5,4,3,2,1,0:T(8,128)(2,1)}, bf16[1,2,4,2,128,128]{5,4,3,2,1,0:T(8,128)(2,1)}, bf16[1,2,4,2,128,128]{5,4,3,2,1,0:T(8,128)(2,1)},...) custom-call(s32[12]{0:T(128)} %stack.79.shard_ref, ...), custom_call_target="tpu_custom_call" | custom-call | bytes 16800000 | tf_op jit(solution)/shard_map/pack/pallas_call | solution.py:242
  47.1 1.9 collective-permute-start.16
  49.0 4.5 %collective-permute-done.14.refs_0_ = bf16[1,2,4,2,128,128]{5,4,3,2,1,0:T(8,128)(2,1)S(1)} collective-permute-done((bf16[1,2,4,2,128,128]{5,4,3,2,1,0:T(8,128)(2,1)}, bf16[1,2,4,2,128,128]{5,4,3,2,1,0:T(8,128)(2,1)S(1)}, u32[]{:S(2)}, u32[]{:S(2)}) %collective-permute-start.14) | collective-permute-done | bytes 524320 | tf_op jit(solution)/shard_map/ppermute | solution.py:29
  56.5 8.3 %collective-permute-done.15.refs_1_ = bf16[1,2,4,2,128,128]{5,4,3,2,1,0:T(8,128)(2,1)S(1)} collective-permute-done((bf16[1,2,4,2,128,128]{5,4,3,2,1,0:T(8,128)(2,1)}, bf16[1,2,4,2,128,128]{5,4,3,2,1,0:T(8,128)(2,1)S(1)}, u32[]{:S(2)}, u32[]{:S(2)}) %collective-permute-start.15) | collective-permute-done | bytes 524320 | tf_op jit(solution)/shard_map/ppermute | solution.py:29
  66.2 11.2 %collective-permute-done.16.refs_2_ = bf16[1,2,4,2,128,128]{5,4,3,2,1,0:T(8,128)(2,1)S(1)} collective-permute-done((bf16[1,2,4,2,128,128]{5,4,3,2,1,0:T(8,128)(2,1)}, bf16[1,2,4,2,128,128]{5,4,3,2,1,0:T(8,128)(2,1)S(1)}, u32[]{:S(2)}, u32[]{:S(2)}) %collective-permute-start.16) | collective-permute-done | bytes 524320 | tf_op jit(solution)/shard_map/ppermute | solution.py:29
  78.9 21.0 %collective-permute-done.23.refs_9_.refs_8_ = bf16[2,4,256,256]{3,2,1,0:T(8,128)(2,1)S(1)} collective-permute-done((bf16[2,4,256,256]{3,2,1,0:T(8,128)(2,1)S(1)}, bf16[2,4,256,256]{3,2,1,0:T(8,128)(2,1)S(1)}, u32[]{:S(2)}, u32[]{:S(2)}) %collective-permute-start.23) | collective-permute-done | bytes 1048608 | tf_op jit(solution)/shard_map/ppermute | solution.py:29
  100.7 13.2 %collective-permute-done.24.refs_10_.refs_9_ = bf16[2,4,256,256]{3,2,1,0:T(8,128)(2,1)S(1)} collective-permute-done((bf16[2,4,256,256]{3,2,1,0:T(8,128)(2,1)S(1)}, bf16[2,4,256,256]{3,2,1,0:T(8,128)(2,1)S(1)}, u32[]{:S(2)}, u32[]{:S(2)}) %collective-permute-start.24) | collective-permute-done | bytes 1048608 | tf_op jit(solution)/shard_map/ppermute | solution.py:29
  115.8 20.7 %collective-permute-done.29.refs_0_ = bf16[2,2,4,2,128,128]{5,4,3,2,1,0:T(8,128)(2,1)} collective-permute-done((bf16[2,2,4,2,128,128]{5,4,3,2,1,0:T(8,128)(2,1)}, bf16[2,2,4,2,128,128]{5,4,3,2,1,0:T(8,128)(2,1)}, u32[]{:S(2)}, u32[]{:S(2)}) %collective-permute-start.29) | collective-permute-done | bytes 1048608 | tf_op jit(solution)/shard_map/ppermute | solution.py:29
  136.5 2.0 collective-permute-start.25
  138.5 2.2 collective-permute-start.37
  141.6 15.4 %collective-permute-done.22.refs_7_.refs_6_ = bf16[2,4,256,256]{3,2,1,0:T(8,128)(2,1)S(1)} collective-permute-done((bf16[2,4,256,256]{3,2,1,0:T(8,128)(2,1)}, bf16[2,4,256,256]{3,2,1,0:T(8,128)(2,1)S(1)}, u32[]{:S(2)}, u32[]{:S(2)}) %collective-permute-start.22) | collective-permute-done | bytes 1048608 | tf_op jit(solution)/shard_map/ppermute | solution.py:29
  158.4 14.9 %collective-permute-start.9 = (bf16[2,4,256,256]{3,2,1,0:T(8,128)(2,1)}, bf16[2,4,256,256]{3,2,1,0:T(8,128)(2,1)}, u32[]{:S(2)}, u32[]{:S(2)}) collective-permute-start(bf16[2,4,256,256]{3,2,1,0:T(8,128)(2,1)} %get-tuple-element.44), channel_id=1, source_target_pairs={{0,1},{1,2},{2,3},{3,4},{4,5},{5,6},{6,7},{7,8},{8,9},{9,10},{10,1... | collective-permute-start | bytes 3145736 | tf_op jit(solution)/shard_map/ppermute | solution.py:328
  174.3 11.4 %collective-permute-start.10 = (bf16[2,4,256,256]{3,2,1,0:T(8,128)(2,1)}, bf16[2,4,256,256]{3,2,1,0:T(8,128)(2,1)}, u32[]{:S(2)}, u32[]{:S(2)}) collective-permute-start(bf16[2,4,256,256]{3,2,1,0:T(8,128)(2,1)} %get-tuple-element.43), channel_id=1, source_target_pairs={{1,0},{2,1},{3,2},{4,3},{5,4},{6,5},{7,6},{8,7},{9,8},{10,9},{11,1... | collective-permute-start | bytes 3145736 | tf_op jit(solution)/shard_map/ppermute | solution.py:329
  187.5 5.4 %partial_near.3 = (bf16[2,1,256,256]{3,2,1,0:T(8,128)(2,1)}, bf16[2,1,256,256]{3,2,1,0:T(8,128)(2,1)}, bf16[2,1,256,256]{3,2,1,0:T(8,128)(2,1)}) custom-call(s32[256]{0:T(256)} %copy-done.26, s32[256]{0:T(256)} %copy-done.27, s32[256]{0:T(256)} %copy-done.28, s32[12]{0:T(128)} %stack.69.shard_ref, bf16[1,2,4,2,128,128]{5,4,3,2,1,0:T(8,128)(2,1)} %copy-done.29, ...), custom_call_target="tpu_custom_call" | custom-call | flops 1620000000 | bytes 5700000 | tf_op jit(solution)/shard_map/partial_near/pallas_call | solution.py:98
  192.9 9.0 %partial_near.4 = (bf16[2,2,256,256]{3,2,1,0:T(8,128)(2,1)}, bf16[2,2,256,256]{3,2,1,0:T(8,128)(2,1)}, bf16[2,2,256,256]{3,2,1,0:T(8,128)(2,1)}) custom-call(s32[256]{0:T(256)} %copy-done.26, s32[256]{0:T(256)} %copy-done.27, s32[256]{0:T(256)} %copy-done.28, s32[12]{0:T(128)} %stack.69.shard_ref, ...), custom_call_target="tpu_custom_call" | custom-call | flops 3240000000 | bytes 11400000 | tf_op jit(solution)/shard_map/partial_near/pallas_call | solution.py:98
  203.4 9.7 %partial_near.5 = (bf16[2,2,256,256]{3,2,1,0:T(8,128)(2,1)}, bf16[2,2,256,256]{3,2,1,0:T(8,128)(2,1)}, bf16[2,3,256,256]{3,2,1,0:T(8,128)(2,1)}) custom-call(s32[256]{0:T(256)} %copy-done.26, s32[256]{0:T(256)} %copy-done.27, s32[256]{0:T(256)} %copy-done.28, s32[12]{0:T(128)} %stack.69.shard_ref, ...), custom_call_target="tpu_custom_call" | custom-call | flops 3780000000 | bytes 13300000 | tf_op jit(solution)/shard_map/partial_near/pallas_call | solution.py:98
  215.7 18.3 %couple.1.refs_17_.refs_3_ = bf16[2,16,256,256]{3,2,1,0:T(8,128)(2,1)} custom-call(f32[256,288]{1,0:T(8,128)} %bitcast.20, bf16[2,4,256,256]{3,2,1,0:T(8,128)(2,1)} %collective-permute-done.9.low_ref, bf16[2,16,256,256]{3,2,1,0:T(8,128)(2,1)} %refs_16_.3, bf16[2,4,256,256]{3,2,1,0:T(8,128)(2,1)} %collective-permute-done.10.high_ref), custom_call_target="tpu_custom_call" | custom-call | flops 20000000000 | bytes 10000000 | tf_op jit(solution)/shard_map/couple/pallas_call | solution.py:292
  234.0 6.2 %own_near.2.base_ref = f32[2,3,256,256]{3,2,1,0:T(8,128)} custom-call(s32[256]{0:T(256)} %copy-done.25, s32[12]{0:T(128)} %stack.69.shard_ref, bf16[16,2,8,2,128,128]{5,4,3,2,1,0:T(8,128)(2,1)} %refs_3_.3, bf16[16,2,8,2,128,128]{5,4,3,2,1,0:T(8,128)(2,1)} %refs_3_.3, bf16[16,2,8,2,128,128]{5,4,3,2,1,0:T(8,128)(2,1)} %refs_3_.3, ...), custom_call_target="tpu_custom_call" | custom-call | flops 1620000000 | bytes 7800000 | tf_op jit(solution)/shard_map/own_near/pallas_call | solution.py:148
  240.7 1.6 collective-permute-start.19
  243.8 17.4 %own_near.3.base_ref = f32[2,13,256,256]{3,2,1,0:T(8,128)} custom-call(s32[256]{0:T(256)} %copy-done.25, s32[12]{0:T(128)} %stack.69.shard_ref, bf16[16,2,8,2,128,128]{5,4,3,2,1,0:T(8,128)(2,1)} %refs_3_.3, bf16[16,2,8,2,128,128]{5,4,3,2,1,0:T(8,128)(2,1)} %refs_3_.3, bf16[16,2,8,2,128,128]{5,4,3,2,1,0:T(8,128)(2,1)} %refs_3_.3, ...), custom_call_target="tpu_custom_call" | custom-call | flops 7020000256 | bytes 33800000 | tf_op jit(solution)/shard_map/own_near/pallas_call | solution.py:148
  261.3 4.0 %final_sum.3.refs_3_ = bf16[2,16,256,256]{3,2,1,0:T(8,128)(2,1)} custom-call(f32[2,13,256,256]{3,2,1,0:T(8,128)} %own_near.3.base_ref, bf16[2,2,256,256]{3,2,1,0:T(8,128)(2,1)} %copy-done.17, bf16[2,2,256,256]{3,2,1,0:T(8,128)(2,1)} %copy-done.18, bf16[2,3,256,256]{3,2,1,0:T(8,128)(2,1)} %copy-done.15, ...), custom_call_target="tpu_custom_call", output_to_operand_aliasing={{}: (4, {})} | custom-call | flops 1835008 | bytes 7350000 | tf_op jit(solution)/shard_map/final_sum/pallas_call | solution.py:195
  266.9 3.6 %final_sum.4.refs_3_ = bf16[2,16,256,256]{3,2,1,0:T(8,128)(2,1)} custom-call(f32[2,13,256,256]{3,2,1,0:T(8,128)} %own_near.3.base_ref, bf16[2,2,256,256]{3,2,1,0:T(8,128)(2,1)} %copy-done.16, bf16[2,2,256,256]{3,2,1,0:T(8,128)(2,1)} %copy-done.19, bf16[2,2,256,256]{3,2,1,0:T(8,128)(2,1)} %copy-done.20, ...), custom_call_target="tpu_custom_call", output_to_operand_aliasing={{}: (4, {})} | custom-call | flops 1572864 | bytes 6300000 | tf_op jit(solution)/shard_map/final_sum/pallas_call | solution.py:195
  270.5 2.4 final_sum.5
  (137 shorter events, 30.8 us)
Async XLA Ops:
  1.2 19.5 %collective-permute-start = (bf16[2,1,256,256]{3,2,1,0:T(8,128)(2,1)S(1)}, bf16[2,1,256,256]{3,2,1,0:T(8,128)(2,1)S(1)}, u32[]{:S(2)}, u32[]{:S(2)}) collective-permute-start(bf16[2,1,256,256]{3,2,1,0:T(8,128)(2,1)S(1)} %get-tuple-element.47.refs_4_.refs_3_), channel_id=1, source_target_pairs={{0,32},{32,0},{96,64},{64,96},{16,48},{48,16},{112,80},{80,112},{1... | collective-permute-start | bytes 786440 | tf_op jit(solution)/shard_map/ppermute | solution.py:29
  20.6 24.2 %collective-permute-start.7 = (bf16[2,1,256,256]{3,2,1,0:T(8,128)(2,1)S(1)}, bf16[2,1,256,256]{3,2,1,0:T(8,128)(2,1)}, u32[]{:S(2)}, u32[]{:S(2)}) collective-permute-start(bf16[2,1,256,256]{3,2,1,0:T(8,128)(2,1)S(1)} %get-tuple-element.45.refs_12_.refs_11_), channel_id=1, source_target_pairs={{0,32},{32,0},{96,64},{64,96},{16,48},{48,16},{112,80},{80,112},{1... | collective-permute-start | bytes 786440 | tf_op jit(solution)/shard_map/ppermute | solution.py:29
  20.7 25.5 %collective-permute-start.2 = (bf16[2,1,256,256]{3,2,1,0:T(8,128)(2,1)S(1)}, bf16[2,1,256,256]{3,2,1,0:T(8,128)(2,1)}, u32[]{:S(2)}, u32[]{:S(2)}) collective-permute-start(bf16[2,1,256,256]{3,2,1,0:T(8,128)(2,1)S(1)} %collective-permute-done.refs_5_.refs_4_), channel_id=1, source_target_pairs={{0,96},{32,64},{96,0},{64,32},{16,112},{48,80},{112,16},{80,48},{1... | collective-permute-start | bytes 786440 | tf_op jit(solution)/shard_map/ppermute | solution.py:29
  22.7 24.3 %collective-permute-start.5 = (bf16[2,1,256,256]{3,2,1,0:T(8,128)(2,1)}, bf16[2,1,256,256]{3,2,1,0:T(8,128)(2,1)}, u32[]{:S(2)}, u32[]{:S(2)}) collective-permute-start(bf16[2,1,256,256]{3,2,1,0:T(8,128)(2,1)} %collective-permute-done.3.refs_9_.refs_8_), channel_id=1, source_target_pairs={{0,16},{32,48},{96,112},{64,80},{16,0},{48,32},{112,96},{80,64},{1... | collective-permute-start | bytes 786440 | tf_op jit(solution)/shard_map/ppermute | solution.py:29
  22.9 24.3 %collective-permute-start.8 = (bf16[2,1,256,256]{3,2,1,0:T(8,128)(2,1)}, bf16[2,1,256,256]{3,2,1,0:T(8,128)(2,1)}, u32[]{:S(2)}, u32[]{:S(2)}) collective-permute-start(bf16[2,1,256,256]{3,2,1,0:T(8,128)(2,1)} %collective-permute-done.6.refs_13_.refs_12_), channel_id=1, source_target_pairs={{0,32},{32,0},{96,64},{64,96},{16,48},{48,16},{112,80},{80,112},{1... | collective-permute-start | bytes 786440 | tf_op jit(solution)/shard_map/ppermute | solution.py:29
  28.5 49.3 %collective-permute-start.20 = (bf16[2,4,256,256]{3,2,1,0:T(8,128)(2,1)S(1)}, bf16[2,4,256,256]{3,2,1,0:T(8,128)(2,1)}, u32[]{:S(2)}, u32[]{:S(2)}) collective-permute-start(bf16[2,4,256,256]{3,2,1,0:T(8,128)(2,1)S(1)} %get-tuple-element.42.refs_4_.refs_3_), channel_id=1, source_target_pairs={{0,32},{32,0},{96,64},{64,96},{16,48},{48,16},{112,80},{80,112},{1... | collective-permute-start | bytes 3145736 | tf_op jit(solution)/shard_map/ppermute | solution.py:29
  46.2 32.7 %collective-permute-start.21 = (bf16[2,4,256,256]{3,2,1,0:T(8,128)(2,1)S(1)}, bf16[2,4,256,256]{3,2,1,0:T(8,128)(2,1)S(1)}, u32[]{:S(2)}, u32[]{:S(2)}) collective-permute-start(bf16[2,4,256,256]{3,2,1,0:T(8,128)(2,1)S(1)} %get-tuple-element.42.refs_4_.refs_3_), channel_id=1, source_target_pairs={{0,96},{32,64},{96,0},{64,32},{16,112},{48,80},{112,16},{80,48},{1... | collective-permute-start | bytes 3145736 | tf_op jit(solution)/shard_map/ppermute | solution.py:29
  47.1 30.3 %collective-permute-start.16 = (bf16[1,2,4,2,128,128]{5,4,3,2,1,0:T(8,128)(2,1)}, bf16[1,2,4,2,128,128]{5,4,3,2,1,0:T(8,128)(2,1)S(1)}, u32[]{:S(2)}, u32[]{:S(2)}) collective-permute-start(bf16[1,2,4,2,128,128]{5,4,3,2,1,0:T(8,128)(2,1)} %get-tuple-element.25), channel_id=1, source_target_pairs={{0,96},{32,64},{96,0},{64,32},{16,112},{48,80},{112,16},{80,48},{1... | collective-permute-start | bytes 1572872 | tf_op jit(solution)/shard_map/ppermute | solution.py:29
  54.3 45.5 %collective-permute-start.23 = (bf16[2,4,256,256]{3,2,1,0:T(8,128)(2,1)S(1)}, bf16[2,4,256,256]{3,2,1,0:T(8,128)(2,1)S(1)}, u32[]{:S(2)}, u32[]{:S(2)}) collective-permute-start(bf16[2,4,256,256]{3,2,1,0:T(8,128)(2,1)S(1)} %get-tuple-element.41.refs_8_.refs_7_), channel_id=1, source_target_pairs={{0,96},{32,64},{96,0},{64,32},{16,112},{48,80},{112,16},{80,48},{1... | collective-permute-start | bytes 3145736 | tf_op jit(solution)/shard_map/ppermute | solution.py:29
  64.9 50.0 %collective-permute-start.26 = (bf16[2,5,256,256]{3,2,1,0:T(8,128)(2,1)S(1)}, bf16[2,5,256,256]{3,2,1,0:T(8,128)(2,1)S(1)}, u32[]{:S(2)}, u32[]{:S(2)}) collective-permute-start(bf16[2,5,256,256]{3,2,1,0:T(8,128)(2,1)S(1)} %slice.31.refs_12_.refs_11_), channel_id=1, source_target_pairs={{0,16},{32,48},{96,112},{64,80},{16,0},{48,32},{112,96},{80,64},{1... | collective-permute-start | bytes 3932168 | tf_op jit(solution)/shard_map/ppermute | solution.py:29
  77.4 36.4 %collective-permute-start.24 = (bf16[2,4,256,256]{3,2,1,0:T(8,128)(2,1)S(1)}, bf16[2,4,256,256]{3,2,1,0:T(8,128)(2,1)S(1)}, u32[]{:S(2)}, u32[]{:S(2)}) collective-permute-start(bf16[2,4,256,256]{3,2,1,0:T(8,128)(2,1)S(1)} %get-tuple-element.41.refs_8_.refs_7_), channel_id=1, source_target_pairs={{0,16},{32,48},{96,112},{64,80},{16,0},{48,32},{112,96},{80,64},{1... | collective-permute-start | bytes 3145736 | tf_op jit(solution)/shard_map/ppermute | solution.py:29
  77.8 58.7 %collective-permute-start.29 = (bf16[2,2,4,2,128,128]{5,4,3,2,1,0:T(8,128)(2,1)}, bf16[2,2,4,2,128,128]{5,4,3,2,1,0:T(8,128)(2,1)}, u32[]{:S(2)}, u32[]{:S(2)}) collective-permute-start(bf16[2,2,4,2,128,128]{5,4,3,2,1,0:T(8,128)(2,1)} %get-tuple-element.29), channel_id=1, source_target_pairs={{0,16},{32,48},{96,112},{64,80},{16,0},{48,32},{112,96},{80,64},{1... | collective-permute-start | bytes 3145736 | tf_op jit(solution)/shard_map/ppermute | solution.py:29
  78.9 57.6 %collective-permute-start.30 = (bf16[2,2,4,2,128,128]{5,4,3,2,1,0:T(8,128)(2,1)}, bf16[2,2,4,2,128,128]{5,4,3,2,1,0:T(8,128)(2,1)}, u32[]{:S(2)}, u32[]{:S(2)}) collective-permute-start(bf16[2,2,4,2,128,128]{5,4,3,2,1,0:T(8,128)(2,1)} %get-tuple-element.30), channel_id=1, source_target_pairs={{0,32},{32,0},{96,64},{64,96},{16,48},{48,16},{112,80},{80,112},{1... | collective-permute-start | bytes 3145736 | tf_op jit(solution)/shard_map/ppermute | solution.py:29
  99.9 38.6 %collective-permute-start.31 = (bf16[2,2,4,2,128,128]{5,4,3,2,1,0:T(8,128)(2,1)}, bf16[2,2,4,2,128,128]{5,4,3,2,1,0:T(8,128)(2,1)S(1)}, u32[]{:S(2)}, u32[]{:S(2)}) collective-permute-start(bf16[2,2,4,2,128,128]{5,4,3,2,1,0:T(8,128)(2,1)} %get-tuple-element.31), channel_id=1, source_target_pairs={{0,96},{32,64},{96,0},{64,32},{16,112},{48,80},{112,16},{80,48},{1... | collective-permute-start | bytes 3145736 | tf_op jit(solution)/shard_map/ppermute | solution.py:29
  113.9 27.5 %collective-permute-start.27 = (bf16[2,5,256,256]{3,2,1,0:T(8,128)(2,1)S(1)}, bf16[2,5,256,256]{3,2,1,0:T(8,128)(2,1)S(1)}, u32[]{:S(2)}, u32[]{:S(2)}) collective-permute-start(bf16[2,5,256,256]{3,2,1,0:T(8,128)(2,1)S(1)} %slice.31.refs_12_.refs_11_), channel_id=1, source_target_pairs={{0,32},{32,0},{96,64},{64,96},{16,48},{48,16},{112,80},{80,112},{1... | collective-permute-start | bytes 3932168 | tf_op jit(solution)/shard_map/ppermute | solution.py:29
  114.8 58.4 %collective-permute-start.28 = (bf16[2,5,256,256]{3,2,1,0:T(8,128)(2,1)S(1)}, bf16[2,5,256,256]{3,2,1,0:T(8,128)(2,1)S(1)}, u32[]{:S(2)}, u32[]{:S(2)}) collective-permute-start(bf16[2,5,256,256]{3,2,1,0:T(8,128)(2,1)S(1)} %collective-permute-done.26.refs_13_.refs_12_), channel_id=1, source_target_pairs={{0,32},{32,0},{96,64},{64,96},{16,48},{48,16},{112,80},{80,112},{1... | collective-permute-start | bytes 3932168 | tf_op jit(solution)/shard_map/ppermute | solution.py:29
  136.4 20.6 %collective-permute-start.22 = (bf16[2,4,256,256]{3,2,1,0:T(8,128)(2,1)}, bf16[2,4,256,256]{3,2,1,0:T(8,128)(2,1)S(1)}, u32[]{:S(2)}, u32[]{:S(2)}) collective-permute-start(bf16[2,4,256,256]{3,2,1,0:T(8,128)(2,1)} %collective-permute-done.20.refs_5_.refs_4_), channel_id=1, source_target_pairs={{0,96},{32,64},{96,0},{64,32},{16,112},{48,80},{112,16},{80,48},{1... | collective-permute-start | bytes 3145736 | tf_op jit(solution)/shard_map/ppermute | solution.py:29
  136.5 21.9 %collective-permute-start.25 = (bf16[2,4,256,256]{3,2,1,0:T(8,128)(2,1)S(1)}, bf16[2,4,256,256]{3,2,1,0:T(8,128)(2,1)S(1)}, u32[]{:S(2)}, u32[]{:S(2)}) collective-permute-start(bf16[2,4,256,256]{3,2,1,0:T(8,128)(2,1)S(1)} %collective-permute-done.23.refs_9_.refs_8_), channel_id=1, source_target_pairs={{0,16},{32,48},{96,112},{64,80},{16,0},{48,32},{112,96},{80,64},{1... | collective-permute-start | bytes 3145736 | tf_op jit(solution)/shard_map/ppermute | solution.py:29
  138.5 64.9 %collective-permute-start.37 = (bf16[3,2,4,2,128,128]{5,4,3,2,1,0:T(8,128)(2,1)}, bf16[3,2,4,2,128,128]{5,4,3,2,1,0:T(8,128)(2,1)}, u32[]{:S(2)}, u32[]{:S(2)}) collective-permute-start(bf16[3,2,4,2,128,128]{5,4,3,2,1,0:T(8,128)(2,1)} %get-tuple-element.37), channel_id=1, source_target_pairs={{0,96},{32,64},{96,0},{64,32},{16,112},{48,80},{112,16},{80,48},{1... | collective-permute-start | bytes 4718600 | tf_op jit(solution)/shard_map/ppermute | solution.py:29
  141.4 60.4 %collective-permute-start.35 = (bf16[2,2,4,2,128,128]{5,4,3,2,1,0:T(8,128)(2,1)}, bf16[2,2,4,2,128,128]{5,4,3,2,1,0:T(8,128)(2,1)}, u32[]{:S(2)}, u32[]{:S(2)}) collective-permute-start(bf16[2,2,4,2,128,128]{5,4,3,2,1,0:T(8,128)(2,1)} %get-tuple-element.35), channel_id=1, source_target_pairs={{0,16},{32,48},{96,112},{64,80},{16,0},{48,32},{112,96},{80,64},{1... | collective-permute-start | bytes 3145736 | tf_op jit(solution)/shard_map/ppermute | solution.py:29
  157.0 45.9 %collective-permute-start.36 = (bf16[2,2,4,2,128,128]{5,4,3,2,1,0:T(8,128)(2,1)}, bf16[2,2,4,2,128,128]{5,4,3,2,1,0:T(8,128)(2,1)}, u32[]{:S(2)}, u32[]{:S(2)}) collective-permute-start(bf16[2,2,4,2,128,128]{5,4,3,2,1,0:T(8,128)(2,1)} %get-tuple-element.36), channel_id=1, source_target_pairs={{0,32},{32,0},{96,64},{64,96},{16,48},{48,16},{112,80},{80,112},{1... | collective-permute-start | bytes 3145736 | tf_op jit(solution)/shard_map/ppermute | solution.py:29
  158.4 55.8 %collective-permute-start.9 = (bf16[2,4,256,256]{3,2,1,0:T(8,128)(2,1)}, bf16[2,4,256,256]{3,2,1,0:T(8,128)(2,1)}, u32[]{:S(2)}, u32[]{:S(2)}) collective-permute-start(bf16[2,4,256,256]{3,2,1,0:T(8,128)(2,1)} %get-tuple-element.44), channel_id=1, source_target_pairs={{0,1},{1,2},{2,3},{3,4},{4,5},{5,6},{6,7},{7,8},{8,9},{9,10},{10,1... | collective-permute-start | bytes 3145736 | tf_op jit(solution)/shard_map/ppermute | solution.py:328
  174.3 40.6 %collective-permute-start.10 = (bf16[2,4,256,256]{3,2,1,0:T(8,128)(2,1)}, bf16[2,4,256,256]{3,2,1,0:T(8,128)(2,1)}, u32[]{:S(2)}, u32[]{:S(2)}) collective-permute-start(bf16[2,4,256,256]{3,2,1,0:T(8,128)(2,1)} %get-tuple-element.43), channel_id=1, source_target_pairs={{1,0},{2,1},{3,2},{4,3},{5,4},{6,5},{7,6},{8,7},{9,8},{10,9},{11,1... | collective-permute-start | bytes 3145736 | tf_op jit(solution)/shard_map/ppermute | solution.py:329
  201.9 68.6 %collective-permute-start.17 = (bf16[2,1,256,256]{3,2,1,0:T(8,128)(2,1)}, bf16[2,1,256,256]{3,2,1,0:T(8,128)(2,1)}, u32[]{:S(2)}, u32[]{:S(2)}) collective-permute-start(bf16[2,1,256,256]{3,2,1,0:T(8,128)(2,1)} %get-tuple-element.26), channel_id=1, source_target_pairs={{0,16},{32,48},{96,112},{64,80},{16,0},{48,32},{112,96},{80,64},{1... | collective-permute-start | bytes 786440 | tf_op jit(solution)/shard_map/ppermute | solution.py:29
  202.9 37.2 %collective-permute-start.32 = (bf16[2,2,256,256]{3,2,1,0:T(8,128)(2,1)}, bf16[2,2,256,256]{3,2,1,0:T(8,128)(2,1)S(1)}, u32[]{:S(2)}, u32[]{:S(2)}) collective-permute-start(bf16[2,2,256,256]{3,2,1,0:T(8,128)(2,1)} %get-tuple-element.32), channel_id=1, source_target_pairs={{0,16},{32,48},{96,112},{64,80},{16,0},{48,32},{112,96},{80,64},{1... | collective-permute-start | bytes 1572872 | tf_op jit(solution)/shard_map/ppermute | solution.py:29
  213.1 27.6 %collective-permute-start.38 = (bf16[2,2,256,256]{3,2,1,0:T(8,128)(2,1)}, bf16[2,2,256,256]{3,2,1,0:T(8,128)(2,1)S(1)}, u32[]{:S(2)}, u32[]{:S(2)}) collective-permute-start(bf16[2,2,256,256]{3,2,1,0:T(8,128)(2,1)} %get-tuple-element.38), channel_id=1, source_target_pairs={{0,16},{32,48},{96,112},{64,80},{16,0},{48,32},{112,96},{80,64},{1... | collective-permute-start | bytes 1572872 | tf_op jit(solution)/shard_map/ppermute | solution.py:29
  214.1 28.1 %collective-permute-start.39 = (bf16[2,2,256,256]{3,2,1,0:T(8,128)(2,1)}, bf16[2,2,256,256]{3,2,1,0:T(8,128)(2,1)S(1)}, u32[]{:S(2)}, u32[]{:S(2)}) collective-permute-start(bf16[2,2,256,256]{3,2,1,0:T(8,128)(2,1)} %get-tuple-element.39), channel_id=1, source_target_pairs={{0,32},{32,0},{96,64},{64,96},{16,48},{48,16},{112,80},{80,112},{1... | collective-permute-start | bytes 1572872 | tf_op jit(solution)/shard_map/ppermute | solution.py:29
  214.9 28.1 %collective-permute-start.40 = (bf16[2,3,256,256]{3,2,1,0:T(8,128)(2,1)}, bf16[2,3,256,256]{3,2,1,0:T(8,128)(2,1)S(1)}, u32[]{:S(2)}, u32[]{:S(2)}) collective-permute-start(bf16[2,3,256,256]{3,2,1,0:T(8,128)(2,1)} %get-tuple-element.40), channel_id=1, source_target_pairs={{0,96},{32,64},{96,0},{64,32},{16,112},{48,80},{112,16},{80,48},{1... | collective-permute-start | bytes 2359304 | tf_op jit(solution)/shard_map/ppermute | solution.py:29
  240.2 30.3 %collective-permute-start.18 = (bf16[2,1,256,256]{3,2,1,0:T(8,128)(2,1)}, bf16[2,1,256,256]{3,2,1,0:T(8,128)(2,1)}, u32[]{:S(2)}, u32[]{:S(2)}) collective-permute-start(bf16[2,1,256,256]{3,2,1,0:T(8,128)(2,1)} %get-tuple-element.27), channel_id=1, source_target_pairs={{0,32},{32,0},{96,64},{64,96},{16,48},{48,16},{112,80},{80,112},{1... | collective-permute-start | bytes 786440 | tf_op jit(solution)/shard_map/ppermute | solution.py:29
  240.7 29.8 %collective-permute-start.19 = (bf16[2,1,256,256]{3,2,1,0:T(8,128)(2,1)}, bf16[2,1,256,256]{3,2,1,0:T(8,128)(2,1)}, u32[]{:S(2)}, u32[]{:S(2)}) collective-permute-start(bf16[2,1,256,256]{3,2,1,0:T(8,128)(2,1)} %get-tuple-element.28), channel_id=1, source_target_pairs={{0,96},{32,64},{96,0},{64,32},{16,112},{48,80},{112,16},{80,48},{1... | collective-permute-start | bytes 786440 | tf_op jit(solution)/shard_map/ppermute | solution.py:29
  242.3 23.0 %collective-permute-start.33 = (bf16[2,2,256,256]{3,2,1,0:T(8,128)(2,1)}, bf16[2,2,256,256]{3,2,1,0:T(8,128)(2,1)S(1)}, u32[]{:S(2)}, u32[]{:S(2)}) collective-permute-start(bf16[2,2,256,256]{3,2,1,0:T(8,128)(2,1)} %get-tuple-element.33), channel_id=1, source_target_pairs={{0,32},{32,0},{96,64},{64,96},{16,48},{48,16},{112,80},{80,112},{1... | collective-permute-start | bytes 1572872 | tf_op jit(solution)/shard_map/ppermute | solution.py:29
  243.1 22.3 %collective-permute-start.34 = (bf16[2,2,256,256]{3,2,1,0:T(8,128)(2,1)}, bf16[2,2,256,256]{3,2,1,0:T(8,128)(2,1)S(1)}, u32[]{:S(2)}, u32[]{:S(2)}) collective-permute-start(bf16[2,2,256,256]{3,2,1,0:T(8,128)(2,1)} %get-tuple-element.34), channel_id=1, source_target_pairs={{0,96},{32,64},{96,0},{64,32},{16,112},{48,80},{112,16},{80,48},{1... | collective-permute-start | bytes 1572872 | tf_op jit(solution)/shard_map/ppermute | solution.py:29
  (41 other events, 1261.8 us)
